TPU v7x, 512 devices: a whole 4x4x16 slice. The times are simulated.
512 devices in a mesh: prow: 16 (over y, x), pcol: 32 (over z, core).
Axes of the slice: x: 4, y: 4, z: 16, core: 2. Of those that a mesh axis runs over, the one named last changes fastest.
Arguments:
- factor_tiles: bfloat16 [16, 1024, 1, 16, 1024], P(None, 'pcol', None, 'prow'), may hold values from -0.03125 to 0.03125
- inverse_blocks: bfloat16 [1, 16, 1024, 1024], P(None, 'prow'), may hold values from -1 to 3, as said below
- demand: bfloat16 [16, 1024, 256], P(None, 'pcol'), may hold values from -6 to 6
Outputs:
- solved: bfloat16 [1, 16, 1024, 256], P(None, 'prow')
Inputs may be any that keep to these rules, and one draw needn't show every extreme that they name: `inverse_blocks`: each [1024, 1024] block is lower triangular with a positive diagonal.
All inputs are finite; a program needn't handle non-finite values.
Results may differ from a plain program's by a relative error of at most 0.0075.
Values may be sent and summed in bfloat16 or wider, within the bound.
A program may use at most 64 MiB of HBM per device.

v0:
```python
import jax
import jax.numpy as jnp
from jax import lax
from jax.sharding import PartitionSpec as P


def on_device(factor_tiles, inverse_blocks, demand):
    block_count, slice_rows, col_slots, single, block_width = factor_tiles.shape
    columns = demand.shape[2]
    prow_size = lax.axis_size("prow")
    my_row = lax.axis_index("prow")
    row_tiles = factor_tiles.reshape(block_count, slice_rows, col_slots * block_width)
    inverse = inverse_blocks.reshape(col_slots, block_width, block_width)
    owned_blocks = jnp.zeros((col_slots, block_width, columns), jnp.bfloat16)
    pending = jnp.zeros((block_count, slice_rows, columns), jnp.float32)

    def advance(step_index, carried):
        owned_blocks, pending = carried
        owner_row = step_index % prow_size
        slot_index = step_index // prow_size
        is_owner = my_row == owner_row
        partial_sum = lax.dynamic_index_in_dim(pending, step_index, 0, keepdims=False)
        summed = lax.psum(partial_sum, "prow")
        target = lax.dynamic_index_in_dim(demand, step_index, 0, keepdims=False)
        residual = (target.astype(jnp.float32) - summed).astype(jnp.bfloat16)
        block_inv = lax.dynamic_index_in_dim(inverse, slot_index, 0, keepdims=False)
        apply_running = jnp.zeros((block_width, columns), jnp.float32)
        segment = lax.all_gather(residual, "pcol", axis=0, tiled=True)
        solved = lax.cond(
            is_owner,
            lambda: jnp.dot(block_inv, segment, preferred_element_type=jnp.float32),
            lambda: apply_running,
        ).astype(jnp.bfloat16)
        owned_blocks = jnp.where(
            is_owner,
            lax.dynamic_update_index_in_dim(owned_blocks, solved, slot_index, 0),
            owned_blocks,
        )
        pending = lax.cond(
            is_owner,
            lambda running: running
            + jnp.einsum("krw,wn->krn", row_tiles, solved, preferred_element_type=jnp.float32),
            lambda running: running,
            pending,
        )
        return (owned_blocks, pending)

    owned_blocks, pending = lax.fori_loop(0, block_count, advance, (owned_blocks, pending))
    return owned_blocks.reshape(col_slots, 1, block_width, columns)


def solution(mesh):
    placed = (
        P(None, "pcol", None, "prow", None),
        P(None, "prow", None, None),
        P(None, "pcol", None),
    )
    return jax.shard_map(
        on_device,
        mesh=mesh,
        in_specs=placed,
        out_specs=P(None, "prow", None, None),
        check_vma=False,
    )
```

profile of v0, /device:TPU:1, one launch (start us, length us, event | category | flops | bytes accessed | tf_op | source)
XLA Modules:
  0.0 1639.2 jit_solution(5200162110590774931)
XLA Ops:
  0.1 1638.4 %while.21 = (s32[]{:T(128)}, bf16[1,1024,256]{2,1,0:T(8,128)(2,1)S(1)}, f32[16,32,256]{2,1,0:T(8,128)S(1)}, s32[]{:T(128)}, bf16[16,32,256]{2,1,0:T(8,128)(2,1)}...) while((s32[]{:T(128)}, ...), condition=%wide.region_6.7_spmd.clone, body=%wide.region_0.6_spmd.clone.sunk | while | flops 806256640 | bytes 13320484 | solution.py:48
  0.1 61.6 %psum.16 = f32[32,256]{1,0:T(8,128)S(1)} all-reduce(f32[32,256]{1,0:T(8,128)S(1)} %dynamic-slice_bitcast_fusion.2), channel_id=1, replica_groups=mesh['prow'=16,'pcol'=32] {'prow'}, use_global_device_ids=true, to_apply=%region_1.1 | all-reduce | flops 8192 | bytes 65536 | tf_op jit(solution)/shard_map/while/body/eval_jaxpr/psum | solution.py:23
  62.4 52.0 %all_gather.12 = bf16[1024,256]{1,0:T(8,128)(2,1)S(1)} all-gather(bf16[32,256]{1,0:T(8,128)(2,1)S(1)} %fusion.10), channel_id=1, replica_groups=mesh['prow'=16,'pcol'=32] {'pcol'}, dimensions={0}, use_global_device_ids=true | all-gather | bytes 540672 | tf_op jit(solution)/shard_map/while/body/eval_jaxpr/all_gather | solution.py:28
  120.4 55.8 %psum.16 = f32[32,256]{1,0:T(8,128)S(1)} all-reduce(f32[32,256]{1,0:T(8,128)S(1)} %dynamic-slice_bitcast_fusion.2), channel_id=1, replica_groups=mesh['prow'=16,'pcol'=32] {'prow'}, use_global_device_ids=true, to_apply=%region_1.1 | all-reduce | flops 8192 | bytes 65536 | tf_op jit(solution)/shard_map/while/body/eval_jaxpr/psum | solution.py:23
  176.9 42.0 %all_gather.12 = bf16[1024,256]{1,0:T(8,128)(2,1)S(1)} all-gather(bf16[32,256]{1,0:T(8,128)(2,1)S(1)} %fusion.10), channel_id=1, replica_groups=mesh['prow'=16,'pcol'=32] {'pcol'}, dimensions={0}, use_global_device_ids=true | all-gather | bytes 540672 | tf_op jit(solution)/shard_map/while/body/eval_jaxpr/all_gather | solution.py:28
  220.5 58.3 %psum.16 = f32[32,256]{1,0:T(8,128)S(1)} all-reduce(f32[32,256]{1,0:T(8,128)S(1)} %dynamic-slice_bitcast_fusion.2), channel_id=1, replica_groups=mesh['prow'=16,'pcol'=32] {'prow'}, use_global_device_ids=true, to_apply=%region_1.1 | all-reduce | flops 8192 | bytes 65536 | tf_op jit(solution)/shard_map/while/body/eval_jaxpr/psum | solution.py:23
  279.5 44.1 %all_gather.12 = bf16[1024,256]{1,0:T(8,128)(2,1)S(1)} all-gather(bf16[32,256]{1,0:T(8,128)(2,1)S(1)} %fusion.10), channel_id=1, replica_groups=mesh['prow'=16,'pcol'=32] {'pcol'}, dimensions={0}, use_global_device_ids=true | all-gather | bytes 540672 | tf_op jit(solution)/shard_map/while/body/eval_jaxpr/all_gather | solution.py:28
  325.3 55.8 %psum.16 = f32[32,256]{1,0:T(8,128)S(1)} all-reduce(f32[32,256]{1,0:T(8,128)S(1)} %dynamic-slice_bitcast_fusion.2), channel_id=1, replica_groups=mesh['prow'=16,'pcol'=32] {'prow'}, use_global_device_ids=true, to_apply=%region_1.1 | all-reduce | flops 8192 | bytes 65536 | tf_op jit(solution)/shard_map/while/body/eval_jaxpr/psum | solution.py:23
  381.8 42.0 %all_gather.12 = bf16[1024,256]{1,0:T(8,128)(2,1)S(1)} all-gather(bf16[32,256]{1,0:T(8,128)(2,1)S(1)} %fusion.10), channel_id=1, replica_groups=mesh['prow'=16,'pcol'=32] {'pcol'}, dimensions={0}, use_global_device_ids=true | all-gather | bytes 540672 | tf_op jit(solution)/shard_map/while/body/eval_jaxpr/all_gather | solution.py:28
  425.4 55.8 %psum.16 = f32[32,256]{1,0:T(8,128)S(1)} all-reduce(f32[32,256]{1,0:T(8,128)S(1)} %dynamic-slice_bitcast_fusion.2), channel_id=1, replica_groups=mesh['prow'=16,'pcol'=32] {'prow'}, use_global_device_ids=true, to_apply=%region_1.1 | all-reduce | flops 8192 | bytes 65536 | tf_op jit(solution)/shard_map/while/body/eval_jaxpr/psum | solution.py:23
  481.9 43.9 %all_gather.12 = bf16[1024,256]{1,0:T(8,128)(2,1)S(1)} all-gather(bf16[32,256]{1,0:T(8,128)(2,1)S(1)} %fusion.10), channel_id=1, replica_groups=mesh['prow'=16,'pcol'=32] {'pcol'}, dimensions={0}, use_global_device_ids=true | all-gather | bytes 540672 | tf_op jit(solution)/shard_map/while/body/eval_jaxpr/all_gather | solution.py:28
  527.5 55.8 %psum.16 = f32[32,256]{1,0:T(8,128)S(1)} all-reduce(f32[32,256]{1,0:T(8,128)S(1)} %dynamic-slice_bitcast_fusion.2), channel_id=1, replica_groups=mesh['prow'=16,'pcol'=32] {'prow'}, use_global_device_ids=true, to_apply=%region_1.1 | all-reduce | flops 8192 | bytes 65536 | tf_op jit(solution)/shard_map/while/body/eval_jaxpr/psum | solution.py:23
  584.0 42.0 %all_gather.12 = bf16[1024,256]{1,0:T(8,128)(2,1)S(1)} all-gather(bf16[32,256]{1,0:T(8,128)(2,1)S(1)} %fusion.10), channel_id=1, replica_groups=mesh['prow'=16,'pcol'=32] {'pcol'}, dimensions={0}, use_global_device_ids=true | all-gather | bytes 540672 | tf_op jit(solution)/shard_map/while/body/eval_jaxpr/all_gather | solution.py:28
  627.6 55.8 %psum.16 = f32[32,256]{1,0:T(8,128)S(1)} all-reduce(f32[32,256]{1,0:T(8,128)S(1)} %dynamic-slice_bitcast_fusion.2), channel_id=1, replica_groups=mesh['prow'=16,'pcol'=32] {'prow'}, use_global_device_ids=true, to_apply=%region_1.1 | all-reduce | flops 8192 | bytes 65536 | tf_op jit(solution)/shard_map/while/body/eval_jaxpr/psum | solution.py:23
  684.1 43.9 %all_gather.12 = bf16[1024,256]{1,0:T(8,128)(2,1)S(1)} all-gather(bf16[32,256]{1,0:T(8,128)(2,1)S(1)} %fusion.10), channel_id=1, replica_groups=mesh['prow'=16,'pcol'=32] {'pcol'}, dimensions={0}, use_global_device_ids=true | all-gather | bytes 540672 | tf_op jit(solution)/shard_map/while/body/eval_jaxpr/all_gather | solution.py:28
  729.7 55.8 %psum.16 = f32[32,256]{1,0:T(8,128)S(1)} all-reduce(f32[32,256]{1,0:T(8,128)S(1)} %dynamic-slice_bitcast_fusion.2), channel_id=1, replica_groups=mesh['prow'=16,'pcol'=32] {'prow'}, use_global_device_ids=true, to_apply=%region_1.1 | all-reduce | flops 8192 | bytes 65536 | tf_op jit(solution)/shard_map/while/body/eval_jaxpr/psum | solution.py:23
  786.1 42.0 %all_gather.12 = bf16[1024,256]{1,0:T(8,128)(2,1)S(1)} all-gather(bf16[32,256]{1,0:T(8,128)(2,1)S(1)} %fusion.10), channel_id=1, replica_groups=mesh['prow'=16,'pcol'=32] {'pcol'}, dimensions={0}, use_global_device_ids=true | all-gather | bytes 540672 | tf_op jit(solution)/shard_map/while/body/eval_jaxpr/all_gather | solution.py:28
  829.8 55.8 %psum.16 = f32[32,256]{1,0:T(8,128)S(1)} all-reduce(f32[32,256]{1,0:T(8,128)S(1)} %dynamic-slice_bitcast_fusion.2), channel_id=1, replica_groups=mesh['prow'=16,'pcol'=32] {'prow'}, use_global_device_ids=true, to_apply=%region_1.1 | all-reduce | flops 8192 | bytes 65536 | tf_op jit(solution)/shard_map/while/body/eval_jaxpr/psum | solution.py:23
  886.3 43.9 %all_gather.12 = bf16[1024,256]{1,0:T(8,128)(2,1)S(1)} all-gather(bf16[32,256]{1,0:T(8,128)(2,1)S(1)} %fusion.10), channel_id=1, replica_groups=mesh['prow'=16,'pcol'=32] {'pcol'}, dimensions={0}, use_global_device_ids=true | all-gather | bytes 540672 | tf_op jit(solution)/shard_map/while/body/eval_jaxpr/all_gather | solution.py:28
  931.8 55.8 %psum.16 = f32[32,256]{1,0:T(8,128)S(1)} all-reduce(f32[32,256]{1,0:T(8,128)S(1)} %dynamic-slice_bitcast_fusion.2), channel_id=1, replica_groups=mesh['prow'=16,'pcol'=32] {'prow'}, use_global_device_ids=true, to_apply=%region_1.1 | all-reduce | flops 8192 | bytes 65536 | tf_op jit(solution)/shard_map/while/body/eval_jaxpr/psum | solution.py:23
  988.3 42.0 %all_gather.12 = bf16[1024,256]{1,0:T(8,128)(2,1)S(1)} all-gather(bf16[32,256]{1,0:T(8,128)(2,1)S(1)} %fusion.10), channel_id=1, replica_groups=mesh['prow'=16,'pcol'=32] {'pcol'}, dimensions={0}, use_global_device_ids=true | all-gather | bytes 540672 | tf_op jit(solution)/shard_map/while/body/eval_jaxpr/all_gather | solution.py:28
  1031.9 55.8 %psum.16 = f32[32,256]{1,0:T(8,128)S(1)} all-reduce(f32[32,256]{1,0:T(8,128)S(1)} %dynamic-slice_bitcast_fusion.2), channel_id=1, replica_groups=mesh['prow'=16,'pcol'=32] {'prow'}, use_global_device_ids=true, to_apply=%region_1.1 | all-reduce | flops 8192 | bytes 65536 | tf_op jit(solution)/shard_map/while/body/eval_jaxpr/psum | solution.py:23
  1088.4 43.9 %all_gather.12 = bf16[1024,256]{1,0:T(8,128)(2,1)S(1)} all-gather(bf16[32,256]{1,0:T(8,128)(2,1)S(1)} %fusion.10), channel_id=1, replica_groups=mesh['prow'=16,'pcol'=32] {'pcol'}, dimensions={0}, use_global_device_ids=true | all-gather | bytes 540672 | tf_op jit(solution)/shard_map/while/body/eval_jaxpr/all_gather | solution.py:28
  1134.0 55.8 %psum.16 = f32[32,256]{1,0:T(8,128)S(1)} all-reduce(f32[32,256]{1,0:T(8,128)S(1)} %dynamic-slice_bitcast_fusion.2), channel_id=1, replica_groups=mesh['prow'=16,'pcol'=32] {'prow'}, use_global_device_ids=true, to_apply=%region_1.1 | all-reduce | flops 8192 | bytes 65536 | tf_op jit(solution)/shard_map/while/body/eval_jaxpr/psum | solution.py:23
  1190.5 42.0 %all_gather.12 = bf16[1024,256]{1,0:T(8,128)(2,1)S(1)} all-gather(bf16[32,256]{1,0:T(8,128)(2,1)S(1)} %fusion.10), channel_id=1, replica_groups=mesh['prow'=16,'pcol'=32] {'pcol'}, dimensions={0}, use_global_device_ids=true | all-gather | bytes 540672 | tf_op jit(solution)/shard_map/while/body/eval_jaxpr/all_gather | solution.py:28
  1234.1 55.8 %psum.16 = f32[32,256]{1,0:T(8,128)S(1)} all-reduce(f32[32,256]{1,0:T(8,128)S(1)} %dynamic-slice_bitcast_fusion.2), channel_id=1, replica_groups=mesh['prow'=16,'pcol'=32] {'prow'}, use_global_device_ids=true, to_apply=%region_1.1 | all-reduce | flops 8192 | bytes 65536 | tf_op jit(solution)/shard_map/while/body/eval_jaxpr/psum | solution.py:23
  1290.6 43.9 %all_gather.12 = bf16[1024,256]{1,0:T(8,128)(2,1)S(1)} all-gather(bf16[32,256]{1,0:T(8,128)(2,1)S(1)} %fusion.10), channel_id=1, replica_groups=mesh['prow'=16,'pcol'=32] {'pcol'}, dimensions={0}, use_global_device_ids=true | all-gather | bytes 540672 | tf_op jit(solution)/shard_map/while/body/eval_jaxpr/all_gather | solution.py:28
  1336.2 55.8 %psum.16 = f32[32,256]{1,0:T(8,128)S(1)} all-reduce(f32[32,256]{1,0:T(8,128)S(1)} %dynamic-slice_bitcast_fusion.2), channel_id=1, replica_groups=mesh['prow'=16,'pcol'=32] {'prow'}, use_global_device_ids=true, to_apply=%region_1.1 | all-reduce | flops 8192 | bytes 65536 | tf_op jit(solution)/shard_map/while/body/eval_jaxpr/psum | solution.py:23
  1392.7 42.0 %all_gather.12 = bf16[1024,256]{1,0:T(8,128)(2,1)S(1)} all-gather(bf16[32,256]{1,0:T(8,128)(2,1)S(1)} %fusion.10), channel_id=1, replica_groups=mesh['prow'=16,'pcol'=32] {'pcol'}, dimensions={0}, use_global_device_ids=true | all-gather | bytes 540672 | tf_op jit(solution)/shard_map/while/body/eval_jaxpr/all_gather | solution.py:28
  1436.3 55.8 %psum.16 = f32[32,256]{1,0:T(8,128)S(1)} all-reduce(f32[32,256]{1,0:T(8,128)S(1)} %dynamic-slice_bitcast_fusion.2), channel_id=1, replica_groups=mesh['prow'=16,'pcol'=32] {'prow'}, use_global_device_ids=true, to_apply=%region_1.1 | all-reduce | flops 8192 | bytes 65536 | tf_op jit(solution)/shard_map/while/body/eval_jaxpr/psum | solution.py:23
  1492.8 43.9 %all_gather.12 = bf16[1024,256]{1,0:T(8,128)(2,1)S(1)} all-gather(bf16[32,256]{1,0:T(8,128)(2,1)S(1)} %fusion.10), channel_id=1, replica_groups=mesh['prow'=16,'pcol'=32] {'pcol'}, dimensions={0}, use_global_device_ids=true | all-gather | bytes 540672 | tf_op jit(solution)/shard_map/while/body/eval_jaxpr/all_gather | solution.py:28
  1538.4 55.8 %psum.16 = f32[32,256]{1,0:T(8,128)S(1)} all-reduce(f32[32,256]{1,0:T(8,128)S(1)} %dynamic-slice_bitcast_fusion.2), channel_id=1, replica_groups=mesh['prow'=16,'pcol'=32] {'prow'}, use_global_device_ids=true, to_apply=%region_1.1 | all-reduce | flops 8192 | bytes 65536 | tf_op jit(solution)/shard_map/while/body/eval_jaxpr/psum | solution.py:23
  (150 shorter events, 103.3 us)
Async XLA Ops:
  114.4 4.2 copy-start
  218.8 1.4 copy-start
  323.6 1.4 copy-start
  423.8 1.4 copy-start
  525.8 1.4 copy-start
  625.9 1.4 copy-start
  728.0 1.4 copy-start
  828.1 1.4 copy-start
  930.2 1.4 copy-start
  1030.3 1.4 copy-start
  1132.3 1.4 copy-start
  1232.5 1.4 copy-start
  1334.5 1.4 copy-start
  1434.6 1.4 copy-start
  1536.7 1.4 copy-start
  1636.8 1.4 copy-start
  1638.4 0.8 copy-start.1
where the time goes:
time: 1640 us
  blocking collectives  1600 us (98%)
  local copies, waits for them, and re-layouts  23 us (1%)
    psum x16, blocking collectives, advance(): summed = lax.psum(partial_sum, 'prow')  901 us
    all_gather x16, blocking collectives, advance(): segment = lax.all_gather(residual, 'pcol', axis=0, tiled=True)  695 us

commit v1 on v0

--- a/solution.py
+++ b/solution.py
@@ -20,7 +20,9 @@
         slot_index = step_index // prow_size
         is_owner = my_row == owner_row
         partial_sum = lax.dynamic_index_in_dim(pending, step_index, 0, keepdims=False)
-        summed = lax.psum(partial_sum, "prow")
+        summed = partial_sum
+        for hop in (1, 2, 4, 8):
+            summed = summed + lax.ppermute(summed, "prow", [(dev, dev ^ hop) for dev in range(16)])
         target = lax.dynamic_index_in_dim(demand, step_index, 0, keepdims=False)
         residual = (target.astype(jnp.float32) - summed).astype(jnp.bfloat16)
         block_inv = lax.dynamic_index_in_dim(inverse, slot_index, 0, keepdims=False)

time: 1640 us -> 971 us (0.59)
  blocking collectives: 1600 us -> 540 us
  starting transfers between devices: 0 us -> 238 us
  waiting for transfers between devices: 0 us -> 141 us
    psum x16 -> x0, blocking collectives: 901 us -> none  [advance(): summed = lax.psum(partial_sum, 'prow')]
    ppermute x0 -> x64, starting transfers between devices: none -> 238 us  [advance(): lax.ppermute(summed, 'prow', [(dev, dev ^ hop) for dev in range(16)])]
    all_gather x16, blocking collectives: 695 us -> 540 us  [advance(): segment = lax.all_gather(residual, 'pcol', axis=0, tiled=True)]
    ppermute x0 -> x64, waiting for transfers between devices: none -> 141 us  [advance(): lax.ppermute(summed, 'prow', [(dev, dev ^ hop) for dev in range(16)])]
  transfers between devices with their start and end apart: 0 -> 64, of which waited for: 0 -> 64; matrix products, arithmetic and copies ran while one was open for 0% -> 0% of each run, Pallas kernels for 0% -> 0%
where the time goes in v1:
time: 971 us; the launch traced here: 963 us
  blocking collectives  540 us (56%)
  starting transfers between devices  238 us (25%)
  waiting for transfers between devices  141 us (15%)
  local copies, waits for them, and re-layouts  23 us (2%)
  other arithmetic  15.1 us (2%)
    all_gather x16, blocking collectives, advance(): segment = lax.all_gather(residual, 'pcol', axis=0, tiled=True)  540 us
    ppermute x64, starting transfers between devices, advance(): lax.ppermute(summed, 'prow', [(dev, dev ^ hop) for dev in range(16)])  238 us
    ppermute x64, waiting for transfers between devices, advance(): lax.ppermute(summed, 'prow', [(dev, dev ^ hop) for dev in range(16)])  141 us
  transfers between devices with their start and end apart: 64, of which 64 were waited for; matrix products, arithmetic and copies ran while one was open for 0% of the time, Pallas kernels for 0%

profile of v1, /device:TPU:1, one launch (start us, length us, event | category | flops | bytes accessed | tf_op | source)
XLA Modules:
  0.0 963.3 jit_solution(2756588183018549048)
XLA Ops:
  0.1 962.5 %while.21 = (s32[]{:T(128)}, bf16[1,1024,256]{2,1,0:T(8,128)(2,1)S(1)}, f32[16,32,256]{2,1,0:T(8,128)S(1)}, s32[]{:T(128)}, bf16[16,32,256]{2,1,0:T(8,128)(2,1)}...) while((s32[]{:T(128)}, ...), condition=%wide.region_5.6_spmd.clone, body=%wide.region_0.5_spmd.clone.sunk | while | flops 806281216 | bytes 14107088 | solution.py:50
  23.3 42.7 %all_gather.12 = bf16[1024,256]{1,0:T(8,128)(2,1)S(1)} all-gather(bf16[32,256]{1,0:T(8,128)(2,1)S(1)} %fusion.13), channel_id=1, replica_groups=mesh['prow'=16,'pcol'=32] {'pcol'}, dimensions={0}, use_global_device_ids=true | all-gather | bytes 540672 | tf_op jit(solution)/shard_map/while/body/eval_jaxpr/all_gather | solution.py:30
  94.3 32.8 %all_gather.12 = bf16[1024,256]{1,0:T(8,128)(2,1)S(1)} all-gather(bf16[32,256]{1,0:T(8,128)(2,1)S(1)} %fusion.13), channel_id=1, replica_groups=mesh['prow'=16,'pcol'=32] {'pcol'}, dimensions={0}, use_global_device_ids=true | all-gather | bytes 540672 | tf_op jit(solution)/shard_map/while/body/eval_jaxpr/all_gather | solution.py:30
  128.8 5.9 collective-permute-start
  153.7 34.5 %all_gather.12 = bf16[1024,256]{1,0:T(8,128)(2,1)S(1)} all-gather(bf16[32,256]{1,0:T(8,128)(2,1)S(1)} %fusion.13), channel_id=1, replica_groups=mesh['prow'=16,'pcol'=32] {'pcol'}, dimensions={0}, use_global_device_ids=true | all-gather | bytes 540672 | tf_op jit(solution)/shard_map/while/body/eval_jaxpr/all_gather | solution.py:30
  195.1 5.3 collective-permute-start.1
  213.3 32.5 %all_gather.12 = bf16[1024,256]{1,0:T(8,128)(2,1)S(1)} all-gather(bf16[32,256]{1,0:T(8,128)(2,1)S(1)} %fusion.13), channel_id=1, replica_groups=mesh['prow'=16,'pcol'=32] {'pcol'}, dimensions={0}, use_global_device_ids=true | all-gather | bytes 540672 | tf_op jit(solution)/shard_map/while/body/eval_jaxpr/all_gather | solution.py:30
  252.1 8.0 collective-permute-start.1
  273.0 33.9 %all_gather.12 = bf16[1024,256]{1,0:T(8,128)(2,1)S(1)} all-gather(bf16[32,256]{1,0:T(8,128)(2,1)S(1)} %fusion.13), channel_id=1, replica_groups=mesh['prow'=16,'pcol'=32] {'pcol'}, dimensions={0}, use_global_device_ids=true | all-gather | bytes 540672 | tf_op jit(solution)/shard_map/while/body/eval_jaxpr/all_gather | solution.py:30
  313.2 5.8 collective-permute-start.1
  333.5 32.5 %all_gather.12 = bf16[1024,256]{1,0:T(8,128)(2,1)S(1)} all-gather(bf16[32,256]{1,0:T(8,128)(2,1)S(1)} %fusion.13), channel_id=1, replica_groups=mesh['prow'=16,'pcol'=32] {'pcol'}, dimensions={0}, use_global_device_ids=true | all-gather | bytes 540672 | tf_op jit(solution)/shard_map/while/body/eval_jaxpr/all_gather | solution.py:30
  378.5 6.2 collective-permute-start.2
  392.9 34.2 %all_gather.12 = bf16[1024,256]{1,0:T(8,128)(2,1)S(1)} all-gather(bf16[32,256]{1,0:T(8,128)(2,1)S(1)} %fusion.13), channel_id=1, replica_groups=mesh['prow'=16,'pcol'=32] {'pcol'}, dimensions={0}, use_global_device_ids=true | all-gather | bytes 540672 | tf_op jit(solution)/shard_map/while/body/eval_jaxpr/all_gather | solution.py:30
  452.4 32.2 %all_gather.12 = bf16[1024,256]{1,0:T(8,128)(2,1)S(1)} all-gather(bf16[32,256]{1,0:T(8,128)(2,1)S(1)} %fusion.13), channel_id=1, replica_groups=mesh['prow'=16,'pcol'=32] {'pcol'}, dimensions={0}, use_global_device_ids=true | all-gather | bytes 540672 | tf_op jit(solution)/shard_map/while/body/eval_jaxpr/all_gather | solution.py:30
  497.4 6.2 collective-permute-start.2
  511.8 33.9 %all_gather.12 = bf16[1024,256]{1,0:T(8,128)(2,1)S(1)} all-gather(bf16[32,256]{1,0:T(8,128)(2,1)S(1)} %fusion.13), channel_id=1, replica_groups=mesh['prow'=16,'pcol'=32] {'pcol'}, dimensions={0}, use_global_device_ids=true | all-gather | bytes 540672 | tf_op jit(solution)/shard_map/while/body/eval_jaxpr/all_gather | solution.py:30
  552.1 5.4 collective-permute-start.1
  570.9 32.4 %all_gather.12 = bf16[1024,256]{1,0:T(8,128)(2,1)S(1)} all-gather(bf16[32,256]{1,0:T(8,128)(2,1)S(1)} %fusion.13), channel_id=1, replica_groups=mesh['prow'=16,'pcol'=32] {'pcol'}, dimensions={0}, use_global_device_ids=true | all-gather | bytes 540672 | tf_op jit(solution)/shard_map/while/body/eval_jaxpr/all_gather | solution.py:30
  620.6 8.0 collective-permute-start.3
  630.5 33.9 %all_gather.12 = bf16[1024,256]{1,0:T(8,128)(2,1)S(1)} all-gather(bf16[32,256]{1,0:T(8,128)(2,1)S(1)} %fusion.13), channel_id=1, replica_groups=mesh['prow'=16,'pcol'=32] {'pcol'}, dimensions={0}, use_global_device_ids=true | all-gather | bytes 540672 | tf_op jit(solution)/shard_map/while/body/eval_jaxpr/all_gather | solution.py:30
  682.2 5.6 collective-permute-start.3
  689.8 32.2 %all_gather.12 = bf16[1024,256]{1,0:T(8,128)(2,1)S(1)} all-gather(bf16[32,256]{1,0:T(8,128)(2,1)S(1)} %fusion.13), channel_id=1, replica_groups=mesh['prow'=16,'pcol'=32] {'pcol'}, dimensions={0}, use_global_device_ids=true | all-gather | bytes 540672 | tf_op jit(solution)/shard_map/while/body/eval_jaxpr/all_gather | solution.py:30
  728.4 5.2 collective-permute-start.1
  739.5 7.7 collective-permute-start.3
  749.2 33.9 %all_gather.12 = bf16[1024,256]{1,0:T(8,128)(2,1)S(1)} all-gather(bf16[32,256]{1,0:T(8,128)(2,1)S(1)} %fusion.13), channel_id=1, replica_groups=mesh['prow'=16,'pcol'=32] {'pcol'}, dimensions={0}, use_global_device_ids=true | all-gather | bytes 540672 | tf_op jit(solution)/shard_map/while/body/eval_jaxpr/all_gather | solution.py:30
  789.4 5.8 collective-permute-start.1
  801.1 6.8 collective-permute-start.3
  810.1 32.2 %all_gather.12 = bf16[1024,256]{1,0:T(8,128)(2,1)S(1)} all-gather(bf16[32,256]{1,0:T(8,128)(2,1)S(1)} %fusion.13), channel_id=1, replica_groups=mesh['prow'=16,'pcol'=32] {'pcol'}, dimensions={0}, use_global_device_ids=true | all-gather | bytes 540672 | tf_op jit(solution)/shard_map/while/body/eval_jaxpr/all_gather | solution.py:30
  859.4 8.0 collective-permute-start.3
  869.4 33.9 %all_gather.12 = bf16[1024,256]{1,0:T(8,128)(2,1)S(1)} all-gather(bf16[32,256]{1,0:T(8,128)(2,1)S(1)} %fusion.13), channel_id=1, replica_groups=mesh['prow'=16,'pcol'=32] {'pcol'}, dimensions={0}, use_global_device_ids=true | all-gather | bytes 540672 | tf_op jit(solution)/shard_map/while/body/eval_jaxpr/all_gather | solution.py:30
  920.7 6.2 collective-permute-start.3
  929.0 31.9 %all_gather.12 = bf16[1024,256]{1,0:T(8,128)(2,1)S(1)} all-gather(bf16[32,256]{1,0:T(8,128)(2,1)S(1)} %fusion.13), channel_id=1, replica_groups=mesh['prow'=16,'pcol'=32] {'pcol'}, dimensions={0}, use_global_device_ids=true | all-gather | bytes 540672 | tf_op jit(solution)/shard_map/while/body/eval_jaxpr/all_gather | solution.py:30
  (310 shorter events, 344.9 us)
Async XLA Ops:
  5.3 6.2 collective-permute-start.1
  16.2 6.4 collective-permute-start.3
  76.6 6.2 collective-permute-start.1
  128.8 7.2 collective-permute-start
  146.9 6.2 collective-permute-start.3
  195.1 6.6 collective-permute-start.1
  206.4 6.2 collective-permute-start.3
  252.1 9.3 collective-permute-start.1
  266.1 6.2 collective-permute-start.3
  313.2 7.1 collective-permute-start.1
  320.3 6.3 collective-permute-start.2
  326.6 6.2 collective-permute-start.3
  372.3 6.2 collective-permute-start.1
  378.5 7.5 collective-permute-start.2
  386.0 6.2 collective-permute-start.3
  433.7 6.2 collective-permute-start.1
  445.6 6.2 collective-permute-start.3
  491.0 6.4 collective-permute-start.1
  497.4 7.5 collective-permute-start.2
  505.0 6.2 collective-permute-start.3
  552.1 6.7 collective-permute-start.1
  564.1 6.2 collective-permute-start.3
  609.7 6.2 collective-permute-start.1
  620.6 9.3 collective-permute-start.3
  671.4 6.2 collective-permute-start.1
  682.2 6.9 collective-permute-start.3
  728.4 6.5 collective-permute-start.1
  739.5 9.0 collective-permute-start.3
  789.4 7.1 collective-permute-start.1
  801.1 8.2 collective-permute-start.3
  859.4 9.3 collective-permute-start.3
  920.7 7.5 collective-permute-start.3
  (49 other events, 185.5 us)
